TPU v7x, 512 devices: a whole 4x4x16 slice. The times are simulated.
512 devices in a mesh: sp: 8 (over z_lo, core), dp: 64 (over z_hi, y, x).
Axes of the slice: x: 4, y: 4, z: 16 (z_hi: 4, z_lo: 4; z = z_hi * 4 + z_lo), core: 2. Of those that a mesh axis runs over, the one named last changes fastest.
Arguments:
- inputs: bfloat16 [512, 8, 8, 8, 128], P('dp', 'sp'), may hold values from -16 to 16
- cotangent: bfloat16 [512, 8, 8, 8, 128], P('dp', 'sp'), may hold values from -6 to 6
- w_conv: bfloat16 [3456, 128], replicated, may hold values from -0.109375 to 0.109375
- w_down: bfloat16 [1024, 256], replicated, may hold values from -0.1875 to 0.1875
- w_up: bfloat16 [2048, 128], replicated, may hold values from -0.375 to 0.375
Outputs:
- grad_input: bfloat16 [512, 8, 8, 8, 128], P('dp', 'sp')
- weight_grads: float32 [966656], P('dp')
All inputs are finite; a program needn't handle non-finite values.
Results may differ from a plain program's by a relative error of at most 0.017.
Values may be sent and summed in bfloat16 or wider, within the bound.
A program may use at most 64 MiB of HBM per device.

v0:
```python
import jax
import jax.numpy as jnp
from jax import lax
from jax.sharding import PartitionSpec as P


def extended(cells, sides, width):
    for axis, dim in sides:
        count = lax.axis_size(axis)
        ends = count - 1
        head = lax.slice_in_dim(cells, 0, width, axis=dim)
        tail = lax.slice_in_dim(cells, cells.shape[dim] - width, cells.shape[dim], axis=dim)
        cells = jnp.concatenate(
            [
                lax.ppermute(tail, axis, [(i, (i + 1) % count) for i in range(ends)]),
                cells,
                lax.ppermute(head, axis, [((i + 1) % count, i) for i in range(ends)]),
            ],
            axis=dim,
        )
    return cells


def silu_slope(pre_act):
    sigmoid_value = jax.nn.sigmoid(pre_act)
    return sigmoid_value * (1.0 + pre_act * (1.0 - sigmoid_value))


def unfold_taps(padded):
    first_size = padded.shape[1] - 2
    second_size = padded.shape[2] - 2
    third_size = padded.shape[3] - 2
    pieces = [
        padded[:, i : i + first_size, j : j + second_size, k : k + third_size, :]
        for i in range(3)
        for j in range(3)
        for k in range(3)
    ]
    stacked = jnp.concatenate(pieces, axis=-1)
    return stacked.reshape(-1, stacked.shape[-1])


def to_blocks(volume):
    shape = volume.shape
    folded = volume.reshape(
        shape[0], shape[1] // 2, 2, shape[2] // 2, 2, shape[3] // 2, 2, shape[4]
    )
    folded = folded.transpose(0, 1, 3, 5, 2, 4, 6, 7)
    return folded.reshape(-1, 8 * shape[4])


def from_blocks(blocked, shape):
    folded = blocked.reshape(
        shape[0], shape[1] // 2, shape[2] // 2, shape[3] // 2, 2, 2, 2, shape[4]
    )
    folded = folded.transpose(0, 1, 4, 2, 5, 3, 6, 7)
    return folded.reshape(shape)


def flip_taps(w_conv):
    width_in = w_conv.shape[1]
    return (
        w_conv.reshape(27, width_in, width_in)[::-1]
        .transpose(0, 2, 1)
        .reshape(27 * width_in, width_in)
    )


def deep_level(hidden, upstream, w_down, w_up):
    width_in = hidden.shape[-1]
    width_deep = w_down.shape[1]
    hid_blocks = to_blocks(hidden)
    up_blocks = to_blocks(upstream)
    pre_deep = jnp.dot(hid_blocks, w_down, preferred_element_type=jnp.float32)
    deep_act = jax.nn.silu(pre_deep).astype(jnp.bfloat16)
    w_up_back = (
        w_up.reshape(8, width_deep, width_in).transpose(0, 2, 1).reshape(8 * width_in, width_deep)
    )
    grad_act = jnp.dot(up_blocks, w_up_back, preferred_element_type=jnp.float32)
    grad_up = lax.dot_general(
        deep_act, up_blocks, (((0,), (0,)), ((), ())), preferred_element_type=jnp.float32
    )
    grad_up = (
        grad_up.reshape(width_deep, 8, width_in)
        .transpose(1, 0, 2)
        .reshape(8 * width_deep, width_in)
    )
    grad_deep = (grad_act * silu_slope(pre_deep)).astype(jnp.bfloat16)
    grad_down = lax.dot_general(
        hid_blocks, grad_deep, (((0,), (0,)), ((), ())), preferred_element_type=jnp.float32
    )
    back_blocks = jnp.dot(grad_deep, w_down.T, preferred_element_type=jnp.float32).astype(
        jnp.bfloat16
    )
    return (grad_down, grad_up, from_blocks(back_blocks, hidden.shape))


def per_device(inputs, cotangent, w_conv, w_down, w_up):
    width_in = w_conv.shape[1]
    edge_pad = ((0, 0), (0, 0), (1, 1), (1, 1), (0, 0))
    slab_in = extended(inputs, (("sp", 1),), 1)
    columns = unfold_taps(jnp.pad(slab_in, edge_pad))
    pre_conv = jnp.dot(columns, w_conv, preferred_element_type=jnp.float32)
    hidden = jax.nn.silu(pre_conv).astype(jnp.bfloat16).reshape(inputs.shape)
    hidden_crops, upstream_crops = (
        lax.all_to_all(hidden, "sp", split_axis=0, concat_axis=1, tiled=True),
        lax.all_to_all(cotangent, "sp", split_axis=0, concat_axis=1, tiled=True),
    )
    grad_down, grad_up, back_down = deep_level(hidden_crops, upstream_crops, w_down, w_up)
    back_slab = lax.all_to_all(back_down, "sp", split_axis=1, concat_axis=0, tiled=True)
    summed = cotangent.astype(jnp.float32).reshape(-1, width_in) + back_slab.astype(
        jnp.float32
    ).reshape(-1, width_in)
    grad_pre = (summed * silu_slope(pre_conv)).astype(jnp.bfloat16)
    grad_conv = lax.dot_general(
        columns, grad_pre, (((0,), (0,)), ((), ())), preferred_element_type=jnp.float32
    )
    padded_grad = extended(grad_pre.reshape(inputs.shape), (("sp", 1),), 1)
    grad_input = jnp.dot(
        unfold_taps(jnp.pad(padded_grad, edge_pad)),
        flip_taps(w_conv),
        preferred_element_type=jnp.float32,
    )
    grad_input = grad_input.astype(jnp.bfloat16).reshape(inputs.shape)
    local_sums = jnp.concatenate(
        [grad_conv.reshape(-1), grad_down.reshape(-1), grad_up.reshape(-1)]
    )
    within_group = lax.psum(local_sums.astype(jnp.bfloat16), "sp").astype(jnp.float32)
    grad_share = lax.psum_scatter(within_group, "dp", scatter_dimension=0, tiled=True)
    edge_cells = inputs.shape[2]
    crop_total = inputs.shape[0] * lax.axis_size("dp")
    norm_factor = 1.0 / jnp.sqrt(jnp.float32(crop_total * edge_cells * edge_cells * edge_cells))
    return (grad_input, grad_share * norm_factor)


def solution(mesh):
    return jax.shard_map(
        per_device,
        mesh=mesh,
        in_specs=(P("dp", "sp", None, None, None), P("dp", "sp", None, None, None), P(), P(), P()),
        out_specs=(P("dp", "sp", None, None, None), P("dp")),
        check_vma=False,
    )
```

profile of v0, /device:TPU:384, one launch (start us, length us, event | category | flops | bytes accessed | tf_op | source)
XLA Modules:
  0.0 712.0 jit_solution(7751137116307948832)
XLA Ops:
  7.2 0.0 copy-start
  7.2 1.9 collective-permute-start
  9.1 1.3 collective-permute-start.1
  10.4 5.7 all-to-all-start
  16.1 0.0 collective-permute-done
  16.1 0.0 collective-permute-done.1
  16.1 1.3 select_maximum_fusion.2
  17.4 0.0 copy-start.2
  17.5 0.1 slice_dynamic-update-slice_fusion.22
  17.6 0.1 slice_dynamic-update-slice_fusion.21
  17.7 0.1 slice_dynamic-update-slice_fusion.19
  17.9 0.1 slice_dynamic-update-slice_fusion.17
  17.9 0.1 slice_dynamic-update-slice_fusion.16
  18.1 0.1 slice_dynamic-update-slice_fusion.14
  18.1 0.1 slice_dynamic-update-slice_fusion.13
  18.3 0.1 slice_dynamic-update-slice_fusion.11
  18.4 0.1 slice_dynamic-update-slice_fusion.9
  18.5 0.1 slice_dynamic-update-slice_fusion.8
  18.6 0.1 slice_dynamic-update-slice_fusion.6
  18.7 0.1 slice_dynamic-update-slice_fusion.5
  18.9 0.0 copy-start.4
  18.9 0.1 slice_dynamic-update-slice_fusion.3
  19.0 0.1 slice_dynamic-update-slice_fusion.1
  19.1 0.1 slice_dynamic-update-slice_fusion
  19.1 1.7 copy-done.1
  20.9 1.8 multiply_convert_fusion
  22.6 0.3 all-to-all-done
  22.9 4.8 all-to-all-start.1
  27.7 0.2 copy.21
  28.0 0.1 copy.35
  28.1 0.1 reshape.112
  28.1 6.4 all-to-all-done.1
  34.5 0.1 copy.23
  34.6 0.1 reshape.118
  34.7 0.2 fusion.23
  34.9 0.2 fusion.8
  35.1 0.3 convolution_convert_fusion.4
  35.4 0.0 copy-start.3
  35.4 0.1 reshape.119
  35.5 0.8 copy.24
  36.3 3.4 all-to-all-start.2
  39.6 0.0 all-reduce.6.cloned.1.call-start
  39.7 0.1 reverse_bitcast_fusion
  39.8 1.3 copy.25
  41.1 1.3 dynamic-slice
  43.0 0.3 fusion.7
  43.3 0.4 copy.29
  43.8 0.3 convolution_convert_fusion.1
  44.1 2.3 all-to-all-done.2
  46.4 0.1 fusion.16
  46.5 3.1 fusion
  49.6 1.4 collective-permute-start.2
  51.1 1.3 collective-permute-start.3
  52.4 1.4 pad_maximum_fusion
  53.8 0.0 all-reduce.6.cloned.1.call-update
  53.8 0.0 collective-permute-done.2
  53.9 1.5 collective-permute-done.3
  55.3 0.4 select_maximum_fusion
  55.7 0.1 fusion.22
  55.8 0.6 fusion.21
  57.5 1.7 convolution_convert_fusion.3
  59.2 85.0 %all-reduce.6.cloned.1.call-done = bf16[966656]{0:T(1024)(128)(2,1)} async-done(((bf16[966656]{0:T(1024)(128)(2,1)}), bf16[966656]{0:T(1024)(128)(2,1)}) %all-reduce.6.cloned.1.call-update) | async-done | bytes 1933328 | tf_op jit(solution)/shard_map/psum | solution.py:128
  144.2 559.4 %all-reduce.7 = f32[966656]{0:T(1024)} all-reduce(bf16[966656]{0:T(1024)(128)(2,1)} %all-reduce.6.cloned.1.call-done), channel_id=2, replica_groups=mesh['sp'=8,'dp'=64] {'dp'}, use_global_device_ids=true, to_apply=%region_1.2.clone | all-reduce | flops 966656 | bytes 5799936
  703.6 1.6 dynamic-slice_multiply_fusion
  (46 shorter events, 1.4 us)
Async XLA Ops:
  7.2 27.5 %copy-start = (bf16[1024,256]{1,0:T(8,128)(2,1)S(1)}, bf16[1024,256]{1,0:T(8,128)(2,1)}, u32[]{:S(2)}) copy-start(bf16[1024,256]{1,0:T(8,128)(2,1)} %param.8) | copy-start | bytes 1572868
  7.2 11.1 %copy-start.5 = (bf16[8,1,8,8,128]{4,3,2,1,0:T(8,128)(2,1)S(1)}, bf16[8,1,8,8,128]{4,3,2,1,0:T(8,128)(2,1)}, u32[]{:S(2)}) copy-start(bf16[8,1,8,8,128]{4,3,2,1,0:T(8,128)(2,1)} %param.5) | copy-start | bytes 393220
  7.2 8.9 %collective-permute-start = (bf16[8,1,8,8,128]{4,3,2,1,0:T(8,128)(2,1)}, bf16[8,1,8,8,128]{4,3,2,1,0:T(8,128)(2,1)S(1)}, u32[]{:S(2)}, u32[]{:S(2)}) collective-permute-start(bf16[8,1,8,8,128]{4,3,2,1,0:T(8,128)(2,1)} %param.5), channel_id=1, source_target_pairs={{0,64},{64,128},{128,192},{192,256},{256,320},{320,384},{384,448},... | collective-permute-start | bytes 393224 | tf_op jit(solution)/shard_map/ppermute | solution.py:15
  9.1 7.0 collective-permute-start.1
  10.4 12.5 %all-to-all-start = ((bf16[8,1,8,8,128]{4,3,2,1,0:T(8,128)(2,1)}), bf16[8,1,8,8,128]{4,3,2,1,0:T(8,128)(2,1)S(1)}, u32[]{:S(2)}, u32[]{:S(2)}) async-start(bf16[8,1,8,8,128]{4,3,2,1,0:T(8,128)(2,1)} %param.6), calls=%async_computation | async-start | bytes 262144 | tf_op jit(solution)/shard_map/all_to_all | solution.py:107
  17.4 3.4 copy-start.2
  18.9 8.9 %copy-start.4 = (bf16[2048,128]{1,0:T(8,128)(2,1)S(1)}, bf16[2048,128]{1,0:T(8,128)(2,1)}, u32[]{:S(2)}) copy-start(bf16[2048,128]{1,0:T(8,128)(2,1)} %param.9) | copy-start | bytes 1572868
  19.1 1.7 copy-start.1
  22.9 11.6 %all-to-all-start.1 = ((bf16[8,1,8,8,128]{4,3,2,1,0:T(8,128)(2,1)}), bf16[8,1,8,8,128]{4,3,2,1,0:T(8,128)(2,1)S(1)}, u32[]{:S(2)}, u32[]{:S(2)}) async-start(bf16[8,1,8,8,128]{4,3,2,1,0:T(8,128)(2,1)} %bitcast.8), calls=%async_computation.1 | async-start | bytes 262144 | tf_op jit(solution)/shard_map/all_to_all | solution.py:106
  35.4 10.9 %copy-start.3 = (bf16[8,1,8,8,128]{4,3,2,1,0:T(8,128)(2,1)S(1)}, bf16[8,1,8,8,128]{4,3,2,1,0:T(8,128)(2,1)}, u32[]{:S(2)}) copy-start(bf16[8,1,8,8,128]{4,3,2,1,0:T(8,128)(2,1)} %param.6) | copy-start | bytes 393220
  36.3 10.1 %all-to-all-start.2 = ((bf16[1,8,8,8,128]{4,3,2,0,1:T(8,128)(2,1)}), bf16[1,8,8,8,128]{4,3,2,0,1:T(8,128)(2,1)S(1)}, u32[]{:S(2)}, u32[]{:S(2)}) async-start(bf16[1,8,8,8,128]{4,3,2,0,1:T(8,128)(2,1)} %bitcast.12), calls=%async_computation.2 | async-start | bytes 262144 | tf_op jit(solution)/shard_map/all_to_all | solution.py:110
  39.6 104.6 %all-reduce.6.cloned.1.call-start = ((), (), s32[]{:S(2)}) async-start(), calls=%async_computation.3 | async-start | bytes 3866624 | tf_op jit(solution)/shard_map/psum | solution.py:128
  49.6 4.2 collective-permute-start.2
  51.1 4.2 collective-permute-start.3
Sparse Core Ops, SparseCore 0:
  54.0 90.2 all-reduce.5
where the time goes:
time: 713 us; the launch traced here: 712 us
  blocking collectives  559 us (78%)
  waiting for transfers between devices  95.4 us (13%)
  starting transfers between devices  19.9 us (3%)
  between operations  15.3 us (2%)
  local copies, waits for them, and re-layouts  9.27 us (1%)
  matrix products  7.99 us (1%)
    unnamed x1, blocking collectives  559 us
    psum x1, waiting for transfers between devices, per_device(): lax.psum(local_sums.astype(jnp.bfloat16), 'sp').astype(jnp.float32)  85 us
  transfers between devices with their start and end apart: 8, of which 5 were waited for; matrix products, arithmetic and copies ran while one was open for 2% of the time, Pallas kernels for 0%

commit v1 on v0

--- a/solution.py
+++ b/solution.py
@@ -125,7 +125,9 @@
     local_sums = jnp.concatenate(
         [grad_conv.reshape(-1), grad_down.reshape(-1), grad_up.reshape(-1)]
     )
-    within_group = lax.psum(local_sums.astype(jnp.bfloat16), "sp").astype(jnp.float32)
+    within_group = jnp.sum(lax.all_gather(local_sums.astype(jnp.bfloat16), "sp"), axis=0).astype(
+        jnp.float32
+    )
     grad_share = lax.psum_scatter(within_group, "dp", scatter_dimension=0, tiled=True)
     edge_cells = inputs.shape[2]
     crop_total = inputs.shape[0] * lax.axis_size("dp")

time: 713 us -> 1020 us (1.43)
  the two profiles are of different devices: /device:TPU:384 before, /device:TPU:128 now
where the time goes in v1:
time: 1020 us
  blocking collectives  557 us (55%)
  waiting for transfers between devices  312 us (31%)
  other arithmetic  83.3 us (8%)
  local copies, waits for them, and re-layouts  24 us (2%)
  starting transfers between devices  23.2 us (2%)
  between operations  15.3 us (2%)
    unnamed x1, blocking collectives  557 us
    all_gather x1, waiting for transfers between devices, per_device(): lax.all_gather(local_sums.astype(jnp.bfloat16), 'sp')  301 us
    reduce_sum x1, other arithmetic, per_device(): jnp.sum(lax.all_gather(local_sums.astype(jnp.bfloat16), 'sp'), axis=0)  42.2 us
    unnamed x1, other arithmetic  36.8 us
  transfers between devices with their start and end apart: 8, of which 4 were waited for; matrix products, arithmetic and copies ran while one was open for 1% of the time, Pallas kernels for 0%

profile of v1, /device:TPU:128, one launch (start us, length us, event | category | flops | bytes accessed | tf_op | source)
XLA Modules:
  0.0 1022.6 jit_solution(653455460941544361)
XLA Ops:
  7.2 0.0 copy-start
  7.2 1.9 collective-permute-start
  9.1 1.3 collective-permute-start.1
  10.4 8.4 all-to-all-start
  18.8 0.0 collective-permute-done
  18.8 1.3 select_maximum_fusion.2
  20.1 0.0 copy-start.2
  20.2 0.1 slice_dynamic-update-slice_fusion.22
  20.3 0.1 slice_dynamic-update-slice_fusion.21
  20.4 0.1 slice_dynamic-update-slice_fusion.19
  20.6 0.1 slice_dynamic-update-slice_fusion.17
  20.6 0.1 slice_dynamic-update-slice_fusion.16
  20.7 0.1 slice_dynamic-update-slice_fusion.14
  20.8 0.1 slice_dynamic-update-slice_fusion.13
  21.0 0.1 slice_dynamic-update-slice_fusion.11
  21.1 0.1 slice_dynamic-update-slice_fusion.9
  21.2 0.1 slice_dynamic-update-slice_fusion.8
  21.3 0.1 slice_dynamic-update-slice_fusion.6
  21.4 0.1 slice_dynamic-update-slice_fusion.5
  21.6 0.0 copy-start.5
  21.6 0.1 slice_dynamic-update-slice_fusion.3
  21.7 0.1 slice_dynamic-update-slice_fusion.1
  21.8 0.1 slice_dynamic-update-slice_fusion
  21.8 1.7 copy-done.1
  23.6 1.8 multiply_convert_fusion
  25.4 0.2 all-to-all-done
  25.6 4.9 all-to-all-start.1
  30.5 0.2 copy.21
  30.7 0.1 copy.38
  30.8 0.1 reshape.154
  30.9 6.4 all-to-all-done.1
  37.3 0.1 copy.23
  37.4 0.1 reshape.160
  37.5 0.2 fusion.24
  37.7 0.0 copy-start.4
  37.7 0.2 fusion.9
  37.9 0.3 convolution_convert_fusion.4
  38.2 0.1 reshape.161
  38.3 0.8 copy.24
  39.0 3.4 all-to-all-start.2
  42.4 0.2 all-gather.3.cloned.1.call-start
  42.6 0.3 fusion.7
  43.0 0.8 copy.30
  43.8 0.3 fusion.8
  44.1 0.2 concatenate.114
  44.3 4.8 all-to-all-done.2
  49.1 1.1 fusion.17
  50.2 3.1 fusion
  53.4 14.1 %copy.37 = bf16[1,1,3456,128]{3,1,2,0:T(2,128)(2,1)S(1)} copy(bf16[1,1,3456,128]{3,2,1,0:T(8,128)(2,1)S(1)} %fusion) | data formatting | bytes 1769472
  67.5 36.8 %maximum_bitcast_fusion = bf16[1,1,966656]{2,1,0:T(2,128)(2,1)} fusion(bf16[1,262144]{1,0:T(2,128)(2,1)S(1)} %concatenate.114, bf16[1,262144]{1,0:T(2,128)(2,1)S(1)} %bitcast.100, bf16[1,442368]{1,0:T(2,128)(2,1)S(1)} %bitcast.99), kind=kLoop, calls=%fused_computation.2 | loop fusion | flops 5799936 | bytes 3866624
  104.3 0.0 all-gather.3.cloned.1.call-update
  104.3 1.6 collective-permute-start.2
  105.9 1.5 collective-permute-start.3
  107.4 0.1 reverse_bitcast_fusion
  107.5 1.3 copy.25
  108.9 1.3 dynamic-slice
  110.8 0.4 select_maximum_fusion
  111.2 0.1 fusion.23
  111.5 0.5 fusion.22
  112.9 1.8 convolution_convert_fusion.3
  114.7 300.6 %all-gather.3.cloned.1.call-done = bf16[8,1,966656]{2,1,0:T(2,128)(2,1)} async-done(((bf16[1,1,966656]{2,1,0:T(2,128)(2,1)}), bf16[8,1,966656]{2,1,0:T(2,128)(2,1)}) %all-gather.3.cloned.1.call-update) | async-done | bytes 15466512 | tf_op jit(solution)/shard_map/all_gather | solution.py:128
  415.3 42.2 %reduce_sum.12 = bf16[966656]{0:T(1024)(128)(2,1)S(1)} reduce(bf16[8,1,966656]{2,1,0:T(2,128)(2,1)} %all-gather.3.cloned.1.call-done, bf16[]{:T(256)} %constant.5.clone.1), dimensions={0,1}, to_apply=%region_0.1 | reduce | flops 6766592 | bytes 17399810 | tf_op jit(solution)/shard_map/reduce_sum | solution.py:128
  457.5 556.7 %all-reduce.4 = f32[966656]{0:T(1024)} all-reduce(bf16[966656]{0:T(1024)(128)(2,1)S(1)} %reduce_sum.12), channel_id=2, replica_groups=mesh['sp'=8,'dp'=64] {'dp'}, use_global_device_ids=true, to_apply=%region_1.2.clone | all-reduce | flops 966656 | bytes 5799936
  1014.2 1.6 dynamic-slice_multiply_fusion
  (51 shorter events, 1.4 us)
Async XLA Ops:
  7.2 30.3 %copy-start = (bf16[1024,256]{1,0:T(8,128)(2,1)S(1)}, bf16[1024,256]{1,0:T(8,128)(2,1)}, u32[]{:S(2)}) copy-start(bf16[1024,256]{1,0:T(8,128)(2,1)} %param.8) | copy-start | bytes 1572868
  7.2 13.8 %copy-start.6 = (bf16[8,1,8,8,128]{4,3,2,1,0:T(8,128)(2,1)S(1)}, bf16[8,1,8,8,128]{4,3,2,1,0:T(8,128)(2,1)}, u32[]{:S(2)}) copy-start(bf16[8,1,8,8,128]{4,3,2,1,0:T(8,128)(2,1)} %param.5) | copy-start | bytes 393220
  7.2 11.6 %collective-permute-start = (bf16[8,1,8,8,128]{4,3,2,1,0:T(8,128)(2,1)}, bf16[8,1,8,8,128]{4,3,2,1,0:T(8,128)(2,1)S(1)}, u32[]{:S(2)}, u32[]{:S(2)}) collective-permute-start(bf16[8,1,8,8,128]{4,3,2,1,0:T(8,128)(2,1)} %param.5), channel_id=1, source_target_pairs={{0,64},{64,128},{128,192},{192,256},{256,320},{320,384},{384,448},... | collective-permute-start | bytes 393224 | tf_op jit(solution)/shard_map/ppermute | solution.py:15
  9.1 9.7 collective-permute-start.1
  10.4 15.2 %all-to-all-start = ((bf16[8,1,8,8,128]{4,3,2,1,0:T(8,128)(2,1)}), bf16[8,1,8,8,128]{4,3,2,1,0:T(8,128)(2,1)S(1)}, u32[]{:S(2)}, u32[]{:S(2)}) async-start(bf16[8,1,8,8,128]{4,3,2,1,0:T(8,128)(2,1)} %param.6), calls=%async_computation | async-start | bytes 262144 | tf_op jit(solution)/shard_map/all_to_all | solution.py:107
  20.1 3.4 copy-start.2
  21.6 9.0 copy-start.5
  21.8 1.8 copy-start.1
  25.6 11.7 %all-to-all-start.1 = ((bf16[8,1,8,8,128]{4,3,2,1,0:T(8,128)(2,1)}), bf16[8,1,8,8,128]{4,3,2,1,0:T(8,128)(2,1)S(1)}, u32[]{:S(2)}, u32[]{:S(2)}) async-start(bf16[8,1,8,8,128]{4,3,2,1,0:T(8,128)(2,1)} %bitcast.8), calls=%async_computation.1 | async-start | bytes 262144 | tf_op jit(solution)/shard_map/all_to_all | solution.py:106
  37.7 11.4 %copy-start.4 = (bf16[8,1,8,8,128]{4,3,2,1,0:T(8,128)(2,1)S(1)}, bf16[8,1,8,8,128]{4,3,2,1,0:T(8,128)(2,1)}, u32[]{:S(2)}) copy-start(bf16[8,1,8,8,128]{4,3,2,1,0:T(8,128)(2,1)} %param.6) | copy-start | bytes 393220
  39.0 10.1 all-to-all-start.2
  42.4 372.9 %all-gather.3.cloned.1.call-start = ((), (), s32[]{:S(2)}) async-start(), calls=%async_computation.3 | async-start | bytes 34799616 | tf_op jit(solution)/shard_map/all_gather | solution.py:128
  104.3 3.1 copy-start.3
  104.3 6.5 collective-permute-start.2
  105.9 4.9 collective-permute-start.3
Sparse Core Ops, SparseCore 0:
  104.4 310.8 all-gather.2
